TPU v7x, 256 devices: a whole 4x4x8 slice. The times are simulated.
256 devices in a mesh: front: 8 (over x, core), grp: 32 (over y, z).
Axes of the slice: x: 4, y: 4, z: 8, core: 2. Of those that a mesh axis runs over, the one named last changes fastest.
Arguments:
- panel_block: bfloat16 [8, 4608, 1024], P('front', 'grp'), may hold values from -0.1796875 to 0.1796875
- trailing: float32 [8, 4608, 4608], P('front', 'grp')
- inverse: float32 [8, 1024, 1024], P('front')
- weights: float32 [8, 4608], P('front'), may hold values from -0.09375 to 0.09375
- live_size: int32 [8], P('front'), may hold values from 2304 to 4608, as said below
- column_source: int32 [8, 4608], P('front'), may hold values from 0 to 4607, each once within a row
- destination: int32 [8, 4608, 1], P('front', 'grp'), may hold values from 0 to 7; in each aligned block of 144 rows (0 to 143, 144 to 287, ..., all dimensions but the last counted through in order) at most 36 rows name the same one
- row_offset: int32 [8, 4608], P('front', 'grp'), may hold values from 0 to 143
Outputs:
- factor: float32 [8, 4608, 1024], P('front', 'grp')
- checksum: float32 [8, 4608], P('front', 'grp')
- ancestor: float32 [8, 4608, 4608], P('front', 'grp')
Inputs may be any that keep to these rules, and one draw needn't show every extreme that they name: `live_size`: each front's live size is 4608 minus a multiple of 576; one front is full. `destination`: among the 144 rows of one device at most 36 rows name the same ancestor front. `column_source`: each front's row is a permutation.
All inputs are finite; a program needn't handle non-finite values.
Results may differ from a plain program's by a relative error of at most 0.0003.
Values may be sent and summed in bfloat16 or wider, within the bound.
A program may use at most 128 MiB of HBM per device.

v0:
```python
import jax
import jax.numpy as jnp
from jax import lax
from jax.sharding import PartitionSpec as P

HIGHEST = lax.Precision.HIGHEST


def bf16_terms(x):
    high = lax.reduce_precision(x, 8, 7)
    rest = x - high
    middle = lax.reduce_precision(rest, 8, 7)
    low = rest - middle
    return [t.astype(jnp.bfloat16) for t in (high, middle, low)]


def on_device(
    panel_block, trailing, inverse, weights, live_size, column_source, destination, row_offset
):
    row_count = trailing.shape[1]
    col_count = trailing.shape[2]
    fronts = lax.axis_size("front")
    capacity = max(2, 2 * row_count // fronts)
    slots = fronts * capacity
    trail_rows = trailing[0]
    inverse_rows = inverse[0]
    live_count = live_size[0]
    panel_all = lax.all_gather(panel_block[0], "grp", axis=0, tiled=True)
    panel_f32 = panel_block[0].astype(jnp.float32)
    factor = jnp.dot(panel_f32, inverse_rows.T, precision=HIGHEST)
    twice = jnp.dot(factor, inverse_rows, precision=HIGHEST)
    rows = jnp.arange(row_count, dtype=jnp.int32)
    live_rows = lax.axis_index("grp") * row_count + rows < live_count
    dest_front = jnp.where(live_rows, destination[0, :, 0], -1)
    earlier = (dest_front[:, None] == dest_front[None, :]) & (rows[None, :] < rows[:, None])
    slot_index = jnp.sum(earlier.astype(jnp.int32), axis=1)
    flat_slot = jnp.where(live_rows, dest_front * capacity + slot_index, -1)
    place = flat_slot[None, :] == jnp.arange(slots, dtype=jnp.int32)[:, None]
    row_tags = jnp.sum(jnp.where(place, row_offset[0][None, :] + 1, 0), axis=1) - 1
    row_tags = row_tags.astype(jnp.float32).reshape(fronts, capacity)
    received_tags = lax.all_to_all(row_tags, "front", split_axis=0, concat_axis=0, tiled=True)
    targets = received_tags.reshape(slots).astype(jnp.int32)
    land = (targets[None, :] == rows[:, None]).astype(jnp.float32)
    source = column_source[0]
    keep = (source < live_count).astype(jnp.float32)
    trail_permuted = jnp.take(trail_rows, source, axis=1)
    kept_weights = jnp.take(weights[0], source) * keep
    update = sum(
        (
            lax.dot_general(
                term, panel_all, (((1,), (1,)), ((), ())), preferred_element_type=jnp.float32
            )
            for term in bf16_terms(twice)
        )
    )
    permuted = (trail_permuted - jnp.take(update, source, axis=1)) * keep[None, :]
    checksum = jnp.dot(permuted, kept_weights, precision=HIGHEST)
    bucket = jnp.dot(place.astype(jnp.float32), permuted, precision=HIGHEST)
    received = lax.all_to_all(
        bucket.reshape(fronts, capacity, col_count),
        "front",
        split_axis=0,
        concat_axis=0,
        tiled=True,
    )
    ancestor = jnp.dot(land, received.reshape(slots, col_count), precision=HIGHEST)
    return (factor[None], checksum[None], ancestor[None])


def solution(mesh):
    placed = (
        P("front", "grp", None),
        P("front", "grp", None),
        P("front", None, None),
        P("front", None),
        P("front"),
        P("front", None),
        P("front", "grp", None),
        P("front", "grp"),
    )
    return jax.shard_map(
        on_device,
        mesh=mesh,
        in_specs=placed,
        out_specs=(P("front", "grp", None), P("front", "grp"), P("front", "grp", None)),
        check_vma=False,
    )
```

profile of v0, /device:TPU:1, one launch (start us, length us, event | category | flops | bytes accessed | tf_op | source)
XLA Modules:
  0.0 257.4 jit_solution(17557925677657125797)
XLA Ops:
  8.6 0.7 fusion.28
  9.5 0.7 broadcast_add_fusion
  10.1 0.7 add_select_fusion
  11.0 0.7 convert_element_type.46
  11.6 6.5 %all-to-all-start = ((f32[8,1,36]{2,1,0:T(1,128)}), f32[8,1,36]{2,1,0:T(1,128)S(1)}, u32[]{:S(2)}, u32[]{:S(2)}) async-start(f32[8,1,36]{2,1,0:T(1,128)} %convert_element_type.46), calls=%async_computation | async-start | bytes 8192 | tf_op jit(solution)/shard_map/all_to_all | solution.py:41
  18.1 5.1 %copy.15 = f32[1,144,4608]{1,2,0:T(8,128)} copy(f32[1,144,4608]{2,1,0:T(8,128)} %param.11) | data formatting | bytes 5308416 | tf_op args[1]
  23.3 14.1 %gather_fusion.1 = f32[4608,144]{1,0:T(8,128)} fusion(f32[144,4608]{0,1:T(8,128)} %bitcast.46, s32[5120]{0:T(1024)S(1)} %pad_clamp_fusion.1), kind=kCustom, calls=%fused_computation.clone | custom fusion | bytes 5326848 | tf_op jit(solution)/shard_map/jit(_take)/gather | solution.py:46
  37.5 4.8 %fusion.15 = f32[144,1024]{1,0:T(8,128)S(1)} fusion(f32[1,1024,1024]{2,1,0:T(8,128)} %param.12, bf16[1,144,1024]{2,1,0:T(8,128)(2,1)S(1)} %copy-done.4), kind=kOutput, calls=%fused_computation.16 | convolution fusion | flops 1811939328 | bytes 5079040 | tf_op jit(solution)/shard_map/dot_general | solution.py:30
  42.3 0.8 copy-done.3
  43.1 2.6 fusion.13
  45.7 71.8 %all-gather.3.cloned.1.call-done = bf16[1,4608,1024]{2,1,0:T(8,128)(2,1)} async-done(((bf16[1,144,1024]{2,1,0:T(8,128)(2,1)}), bf16[1,4608,1024]{2,1,0:T(8,128)(2,1)}) %all-gather.3.cloned.1.call-update) | async-done | bytes 9437200 | tf_op jit(solution)/shard_map/all_gather | solution.py:28
  117.6 7.1 %fusion = f32[144,4608]{1,0:T(8,128)S(1)} fusion(bf16[1,4608,1024]{2,1,0:T(8,128)(2,1)} %all-gather.3.cloned.1.call-done, f32[144,1024]{1,0:T(8,128)S(1)} %fusion.13), kind=kOutput, calls=%fused_computation.3 | convolution fusion | flops 1359691776 | bytes 12681216 | tf_op jit(solution)/shard_map/dot_general | solution.py:50
  124.7 3.3 %fusion.2 = f32[144,4608]{1,0:T(8,128)S(1)} fusion(bf16[1,4608,1024]{2,1,0:T(8,128)(2,1)S(1)} %copy-done.1, f32[144,1024]{1,0:T(8,128)S(1)} %fusion.13), kind=kOutput, calls=%fused_computation.5 | convolution fusion | flops 1359544320 | bytes 12681216 | tf_op jit(solution)/shard_map/dot_general | solution.py:50
  127.9 3.3 %fusion.9 = f32[144,4608]{1,0:T(8,128)S(1)} fusion(f32[144,4608]{1,0:T(8,128)S(1)} %fusion, f32[144,4608]{1,0:T(8,128)S(1)} %fusion.2, bf16[1,4608,1024]{2,1,0:T(8,128)(2,1)S(1)} %copy-done.1, f32[144,1024]{1,0:T(8,128)S(1)} %fusion.13), kind=kOutput, calls=%fused_computation.11 | convolution fusion | flops 1360576512 | bytes 17989632 | tf_op jit(solution)/shard_map/dot_general | solution.py:50
  131.3 3.4 %copy.16 = f32[144,4608]{0,1:T(8,128)} copy(f32[144,4608]{1,0:T(8,128)S(1)} %fusion.9) | data formatting | bytes 5308416 | tf_op jit(solution)/shard_map/add | solution.py:48
  134.6 14.1 %gather_fusion.2 = f32[4608,144]{1,0:T(8,128)} fusion(f32[144,4608]{0,1:T(8,128)} %copy.16, s32[5120]{0:T(1024)S(1)} %pad_clamp_fusion.1), kind=kCustom, calls=%fused_computation.1.clone | custom fusion | bytes 5326848 | tf_op jit(solution)/shard_map/jit(_take)/gather | solution.py:56
  148.8 10.9 %fusion.22 = f32[288,4608]{1,0:T(8,128)} fusion(s32[144]{0:T(256)S(1)} %add_select_fusion, f32[4608,144]{1,0:T(8,128)} %gather_fusion.2, f32[4608,144]{1,0:T(8,128)} %gather_fusion.1, f32[4608]{0:T(1024)S(1)} %fusion.27, pred[4608]{0:T(1024)(128)(4,1)S(1)} %compare_and_fusion), kind=kOutput, calls=%fused_computation.31 | convolution fusion | flops 2295972864 | bytes 10640448 | tf_op jit(solution)/shard_map/dot_general | solution.py:58
  159.7 5.6 %reshape.109 = f32[8,36,4608]{2,1,0:T(8,128)} reshape(f32[288,4608]{1,0:T(8,128)} %fusion.22) | data formatting | bytes 10616832 | tf_op jit(solution)/shard_map/reshape | solution.py:60
  165.3 5.7 %all-to-all-start.1 = ((f32[8,36,4608]{2,1,0:T(8,128)}), f32[8,36,4608]{2,1,0:T(8,128)}, u32[]{:S(2)}, u32[]{:S(2)}) async-start(f32[8,36,4608]{2,1,0:T(8,128)} %reshape.109), calls=%async_computation.1 | async-start | bytes 11796480 | tf_op jit(solution)/shard_map/all_to_all | solution.py:59
  171.1 24.1 %gather_fusion = f32[4608]{0:T(1024)S(1)} fusion(f32[4608]{0:T(1024)S(1)} %reduce.2, s32[5120]{0:T(1024)S(1)} %pad_clamp_fusion), kind=kCustom, calls=%fused_computation.2 | custom fusion | bytes 55296 | tf_op jit(solution)/shard_map/jit(_take)/gather | solution.py:47
  195.3 7.5 %fusion.30 = f32[1,144]{1,0:T(1,128)} fusion(f32[4608,1]{0,1:T(1,128)S(1)} %reshape.143, f32[4608,144]{1,0:T(8,128)} %gather_fusion.2, f32[4608,144]{1,0:T(8,128)} %gather_fusion.1, f32[4608]{0:T(1024)S(1)} %fusion.27, pred[4608]{0:T(1024)(128)(4,1)S(1)} %compare_and_fusion), kind=kOutput, calls=%fused_computation.49 | convolution fusion | flops 10616832 | bytes 5350464 | tf_op jit(solution)/shard_map/dot_general | solution.py:57
  202.8 35.3 %all-to-all-done.1 = f32[8,36,4608]{2,1,0:T(8,128)} async-done(((f32[8,36,4608]{2,1,0:T(8,128)}), f32[8,36,4608]{2,1,0:T(8,128)}, u32[]{:S(2)}, u32[]{:S(2)}) %all-to-all-start.1) | async-done | bytes 5308448 | tf_op jit(solution)/shard_map/all_to_all | solution.py:59
  238.1 5.6 %reshape.110 = f32[288,4608]{1,0:T(8,128)} reshape(f32[8,36,4608]{2,1,0:T(8,128)} %all-to-all-done.1) | data formatting | bytes 10616832 | tf_op jit(solution)/shard_map/reshape | solution.py:66
  243.8 6.8 %convolution_bitcast_fusion = f32[1,144,4608]{2,1,0:T(8,128)} fusion(f32[288,4608]{1,0:T(8,128)} %reshape.110, s32[288]{0:T(512)S(1)} %convert_element_type.48), kind=kOutput, calls=%fused_computation.9 | convolution fusion | flops 2293277184 | bytes 7963776 | tf_op jit(solution)/shard_map/dot_general | solution.py:66
  (29 shorter events, 1.4 us)
Async XLA Ops:
  7.2 163.8 %copy-start = (f32[1,4608]{1,0:T(1,128)S(1)}, f32[1,4608]{1,0:T(1,128)}, u32[]{:S(2)}) copy-start(f32[1,4608]{1,0:T(1,128)} %param.13) | copy-start | bytes 55300
  7.2 16.0 %copy-start.5 = (s32[1,4608]{1,0:T(1,128)S(1)}, s32[1,4608]{1,0:T(1,128)}, u32[]{:S(2)}) copy-start(s32[1,4608]{1,0:T(1,128)} %param.15) | copy-start | bytes 55300
  7.2 110.4 %all-gather.3.cloned.1.call-start = ((), (), s32[]{:S(2)}) async-start(), calls=%async_computation.2 | async-start | bytes 9732096 | tf_op jit(solution)/shard_map/all_gather | solution.py:28
  11.6 153.6 %all-to-all-start = ((f32[8,1,36]{2,1,0:T(1,128)}), f32[8,1,36]{2,1,0:T(1,128)S(1)}, u32[]{:S(2)}, u32[]{:S(2)}) async-start(f32[8,1,36]{2,1,0:T(1,128)} %convert_element_type.46), calls=%async_computation | async-start | bytes 8192 | tf_op jit(solution)/shard_map/all_to_all | solution.py:41
  23.3 14.2 %copy-start.4 = (bf16[1,144,1024]{2,1,0:T(8,128)(2,1)S(1)}, bf16[1,144,1024]{2,1,0:T(8,128)(2,1)}, u32[]{:S(2)}) copy-start(bf16[1,144,1024]{2,1,0:T(8,128)(2,1)} %param.10) | copy-start | bytes 884740
  37.4 5.7 %copy-start.2 = (f32[1,1024,1024]{2,1,0:T(8,128)S(1)}, f32[1,1024,1024]{2,1,0:T(8,128)}, u32[]{:S(2)}) copy-start(f32[1,1024,1024]{2,1,0:T(8,128)} %param.12) | copy-start | bytes 12582916
  42.3 0.8 copy-start.3
  117.6 7.1 %copy-start.1 = (bf16[1,4608,1024]{2,1,0:T(8,128)(2,1)S(1)}, bf16[1,4608,1024]{2,1,0:T(8,128)(2,1)}, u32[]{:S(2)}) copy-start(bf16[1,4608,1024]{2,1,0:T(8,128)(2,1)} %all-gather.3.cloned.1.call-done) | copy-start | bytes 28311556
  165.3 72.9 %all-to-all-start.1 = ((f32[8,36,4608]{2,1,0:T(8,128)}), f32[8,36,4608]{2,1,0:T(8,128)}, u32[]{:S(2)}, u32[]{:S(2)}) async-start(f32[8,36,4608]{2,1,0:T(8,128)} %reshape.109), calls=%async_computation.1 | async-start | bytes 11796480 | tf_op jit(solution)/shard_map/all_to_all | solution.py:59
Sparse Core Ops, SparseCore 0:
  10.6 106.9 all-gather.2
where the time goes:
time: 258 us; the launch traced here: 257 us
  waiting for transfers between devices  108 us (42%)
  local copies, waits for them, and re-layouts  73.7 us (29%)
  matrix products  46.2 us (18%)
  between operations  14.8 us (6%)
  starting transfers between devices  12.2 us (5%)
  other arithmetic  2.64 us (1%)
    all_gather x1, waiting for transfers between devices, on_device(): panel_all = lax.all_gather(panel_block[0], 'grp', axis=0, tiled=True)  71.8 us
    all_to_all x1, waiting for transfers between devices, on_device(): lax.all_to_all(bucket.reshape(fronts, capacity, col_count), 'front', spli...  35.3 us
    gather x1, local copies, waits for them, and re-layouts, on_device(): kept_weights = jnp.take(weights[0], source) * keep  24.1 us
    gather x1, local copies, waits for them, and re-layouts, on_device(): trail_permuted = jnp.take(trail_rows, source, axis=1)  14.1 us
    gather x1, local copies, waits for them, and re-layouts, on_device(): jnp.take(update, source, axis=1)  14.1 us
    dot_general x3, matrix products, on_device(): lax.dot_general(term, panel_all, (((1,), (1,)), ((), ())), preferred_elem...  13.7 us
    dot_general x1, matrix products, on_device(): bucket = jnp.dot(place.astype(jnp.float32), permuted, precision=HIGHEST)  10.9 us
    dot_general x1, matrix products, on_device(): checksum = jnp.dot(permuted, kept_weights, precision=HIGHEST)  7.47 us
  transfers between devices with their start and end apart: 3, of which 2 were waited for; matrix products, arithmetic and copies ran while one was open for 42% of the time, Pallas kernels for 0%

commit v1 on v0

--- a/solution.py
+++ b/solution.py
@@ -4,6 +4,28 @@
 from jax.sharding import PartitionSpec as P
 
 HIGHEST = lax.Precision.HIGHEST
+
+
+def cut_along(x, dim, size):
+    before, after = (x.shape[:dim], x.shape[dim + 1 :])
+    return jnp.moveaxis(x.reshape(*before, size, -1, *after), dim, 0)
+
+
+def laid_out(blocks, dim):
+    lengths = list(blocks.shape[1:])
+    lengths[dim] *= blocks.shape[0]
+    return jnp.moveaxis(blocks, 0, dim).reshape(lengths)
+
+
+def exchange_in_pairs(x, axis, split_dim, concat_dim):
+    length, here = (lax.axis_size(axis), lax.axis_index(axis))
+    blocks = cut_along(x, split_dim, length)
+    outs = [blocks[here]]
+    for step in range(1, length):
+        sent = blocks[here ^ step]
+        outs.append(lax.ppermute(sent, axis, [(i, i ^ step) for i in range(length)]))
+    blocks = jnp.stack(outs)[here ^ jnp.arange(length)]
+    return laid_out(blocks, concat_dim)
 
 
 def bf16_terms(x):
@@ -38,7 +60,7 @@
     place = flat_slot[None, :] == jnp.arange(slots, dtype=jnp.int32)[:, None]
     row_tags = jnp.sum(jnp.where(place, row_offset[0][None, :] + 1, 0), axis=1) - 1
     row_tags = row_tags.astype(jnp.float32).reshape(fronts, capacity)
-    received_tags = lax.all_to_all(row_tags, "front", split_axis=0, concat_axis=0, tiled=True)
+    received_tags = exchange_in_pairs(row_tags, "front", 0, 0)
     targets = received_tags.reshape(slots).astype(jnp.int32)
     land = (targets[None, :] == rows[:, None]).astype(jnp.float32)
     source = column_source[0]

time: 258 us -> 269 us (1.043)
  waiting for transfers between devices: 108 us -> 116 us
  starting transfers between devices: 12.2 us -> 16.5 us
    all_to_all x1, waiting for transfers between devices: 35.3 us -> 0.01 us  [on_device(): lax.all_to_all(bucket.reshape(fronts, capacity, col_count), 'front', spli...]
    ppermute x0 -> x7, waiting for transfers between devices: none -> 34.6 us  [exchange_in_pairs(): lax.ppermute(sent, axis, [(i, i ^ step) for i in range(length)])]
    ppermute x0 -> x7, starting transfers between devices: none -> 10.6 us  [exchange_in_pairs(): lax.ppermute(sent, axis, [(i, i ^ step) for i in range(length)])]
    all_gather x1, waiting for transfers between devices: 71.8 us -> 81.2 us  [on_device(): panel_all = lax.all_gather(panel_block[0], 'grp', axis=0, tiled=True)]
    all_to_all x1 -> x0, starting transfers between devices: 6.45 us -> none  [on_device(): lax.all_to_all(row_tags, 'front', split_axis=0, concat_axis=0, tiled=True)]
    unnamed x13 -> x17, local copies, waits for them, and re-layouts: 5.92 us -> 5.93 us
  transfers between devices with their start and end apart: 3 -> 9, of which waited for: 2 -> 3; matrix products, arithmetic and copies ran while one was open for 42% -> 22% of each run, Pallas kernels for 0% -> 0%
where the time goes in v1:
time: 269 us; the launch traced here: 268 us
  waiting for transfers between devices  116 us (43%)
  local copies, waits for them, and re-layouts  73.7 us (27%)
  matrix products  46.3 us (17%)
  starting transfers between devices  16.5 us (6%)
  between operations  14.9 us (6%)
    all_gather x1, waiting for transfers between devices, on_device(): panel_all = lax.all_gather(panel_block[0], 'grp', axis=0, tiled=True)  81.2 us
    ppermute x7, waiting for transfers between devices, exchange_in_pairs(): lax.ppermute(sent, axis, [(i, i ^ step) for i in range(length)])  34.6 us
    gather x1, local copies, waits for them, and re-layouts, on_device(): kept_weights = jnp.take(weights[0], source) * keep  24.1 us
    gather x1, local copies, waits for them, and re-layouts, on_device(): trail_permuted = jnp.take(trail_rows, source, axis=1)  14.1 us
    gather x1, local copies, waits for them, and re-layouts, on_device(): jnp.take(update, source, axis=1)  14.1 us
    dot_general x3, matrix products, on_device(): lax.dot_general(term, panel_all, (((1,), (1,)), ((), ())), preferred_elem...  13.7 us
    dot_general x1, matrix products, on_device(): bucket = jnp.dot(place.astype(jnp.float32), permuted, precision=HIGHEST)  10.9 us
    ppermute x7, starting transfers between devices, exchange_in_pairs(): lax.ppermute(sent, axis, [(i, i ^ step) for i in range(length)])  10.6 us
  transfers between devices with their start and end apart: 9, of which 3 were waited for; matrix products, arithmetic and copies ran while one was open for 22% of the time, Pallas kernels for 0%

profile of v1, /device:TPU:1, one launch (start us, length us, event | category | flops | bytes accessed | tf_op | source)
XLA Modules:
  0.0 268.5 jit_solution(8887571150105876416)
XLA Ops:
  8.6 5.1 %copy.29 = f32[1,144,4608]{1,2,0:T(8,128)} copy(f32[1,144,4608]{2,1,0:T(8,128)} %param.11) | data formatting | bytes 5308416 | tf_op args[1]
  13.8 14.1 %gather_fusion.2 = f32[4608,144]{1,0:T(8,128)} fusion(f32[144,4608]{0,1:T(8,128)} %bitcast.84, s32[5120]{0:T(1024)S(1)} %pad_clamp_fusion.1), kind=kCustom, calls=%fused_computation.clone | custom fusion | bytes 5326848 | tf_op jit(solution)/shard_map/jit(_take)/gather | solution.py:68
  28.2 4.8 %fusion.15 = f32[144,1024]{1,0:T(8,128)S(1)} fusion(f32[1,1024,1024]{2,1,0:T(8,128)} %param.12, bf16[1,144,1024]{2,1,0:T(8,128)(2,1)S(1)} %copy-done.4), kind=kOutput, calls=%fused_computation.17 | convolution fusion | flops 1811939328 | bytes 5079040 | tf_op jit(solution)/shard_map/dot_general | solution.py:52
  33.0 0.8 copy-done.3
  33.8 2.6 fusion.13
  36.4 81.2 %all-gather.3.cloned.1.call-done = bf16[1,4608,1024]{2,1,0:T(8,128)(2,1)} async-done(((bf16[1,144,1024]{2,1,0:T(8,128)(2,1)}), bf16[1,4608,1024]{2,1,0:T(8,128)(2,1)}) %all-gather.3.cloned.1.call-update) | async-done | bytes 9437200 | tf_op jit(solution)/shard_map/all_gather | solution.py:50
  117.6 7.1 %fusion = f32[144,4608]{1,0:T(8,128)S(1)} fusion(bf16[1,4608,1024]{2,1,0:T(8,128)(2,1)} %all-gather.3.cloned.1.call-done, f32[144,1024]{1,0:T(8,128)S(1)} %fusion.13), kind=kOutput, calls=%fused_computation.4 | convolution fusion | flops 1359691776 | bytes 12681216 | tf_op jit(solution)/shard_map/dot_general | solution.py:72
  124.7 3.3 %fusion.2 = f32[144,4608]{1,0:T(8,128)S(1)} fusion(bf16[1,4608,1024]{2,1,0:T(8,128)(2,1)S(1)} %copy-done.1, f32[144,1024]{1,0:T(8,128)S(1)} %fusion.13), kind=kOutput, calls=%fused_computation.6 | convolution fusion | flops 1359544320 | bytes 12681216 | tf_op jit(solution)/shard_map/dot_general | solution.py:72
  127.9 3.3 %fusion.9 = f32[144,4608]{1,0:T(8,128)S(1)} fusion(f32[144,4608]{1,0:T(8,128)S(1)} %fusion, f32[144,4608]{1,0:T(8,128)S(1)} %fusion.2, bf16[1,4608,1024]{2,1,0:T(8,128)(2,1)S(1)} %copy-done.1, f32[144,1024]{1,0:T(8,128)S(1)} %fusion.13), kind=kOutput, calls=%fused_computation.12 | convolution fusion | flops 1360576512 | bytes 17989632 | tf_op jit(solution)/shard_map/dot_general | solution.py:72
  131.3 3.4 %copy.30 = f32[144,4608]{0,1:T(8,128)} copy(f32[144,4608]{1,0:T(8,128)S(1)} %fusion.9) | data formatting | bytes 5308416 | tf_op jit(solution)/shard_map/add | solution.py:70
  134.7 14.1 %gather_fusion.3 = f32[4608,144]{1,0:T(8,128)} fusion(f32[144,4608]{0,1:T(8,128)} %copy.30, s32[5120]{0:T(1024)S(1)} %pad_clamp_fusion.1), kind=kCustom, calls=%fused_computation.1.clone | custom fusion | bytes 5326848 | tf_op jit(solution)/shard_map/jit(_take)/gather | solution.py:78
  148.8 10.9 %fusion.22 = f32[288,4608]{1,0:T(8,128)} fusion(s32[144]{0:T(256)S(1)} %add_select_fusion, f32[4608,144]{1,0:T(8,128)} %gather_fusion.3, f32[4608,144]{1,0:T(8,128)} %gather_fusion.2, f32[4608]{0:T(1024)S(1)} %fusion.27, pred[4608]{0:T(1024)(128)(4,1)S(1)} %compare_and_fusion), kind=kOutput, calls=%fused_computation.32 | convolution fusion | flops 2295972864 | bytes 10640448 | tf_op jit(solution)/shard_map/dot_general | solution.py:80
  159.6 5.6 %reshape.119 = f32[8,36,4608]{2,1,0:T(8,128)} reshape(f32[288,4608]{1,0:T(8,128)} %fusion.22) | data formatting | bytes 10616832 | tf_op jit(solution)/shard_map/reshape | solution.py:82
  165.2 5.8 %all-to-all-start = ((f32[8,36,4608]{2,1,0:T(8,128)}), f32[8,36,4608]{2,1,0:T(8,128)}, u32[]{:S(2)}, u32[]{:S(2)}) async-start(f32[8,36,4608]{2,1,0:T(8,128)} %reshape.119), calls=%async_computation | async-start | bytes 11796480 | tf_op jit(solution)/shard_map/all_to_all | solution.py:81
  171.5 1.6 collective-permute-start.1
  173.5 2.9 %collective-permute-start.3 = (f32[1,36]{1,0:T(1,128)S(1)}, f32[1,36]{1,0:T(1,128)S(1)}, u32[]{:S(2)}, u32[]{:S(2)}) collective-permute-start(f32[1,36]{1,0:T(1,128)S(1)} %get-tuple-element.7), channel_id=1, source_target_pairs={{0,128},{32,160},{64,192},{96,224},{128,0},{160,32},{192,64},{224,... | collective-permute-start | bytes 440 | tf_op jit(solution)/shard_map/ppermute | solution.py:26
  176.8 24.1 %gather_fusion = f32[4608]{0:T(1024)S(1)} fusion(f32[4608]{0:T(1024)S(1)} %reduce.2, s32[5120]{0:T(1024)S(1)} %pad_clamp_fusion), kind=kCustom, calls=%fused_computation.2 | custom fusion | bytes 55296 | tf_op jit(solution)/shard_map/jit(_take)/gather | solution.py:69
  201.0 2.7 %collective-permute-start.5 = (f32[1,36]{1,0:T(1,128)S(1)}, f32[1,36]{1,0:T(1,128)S(1)}, u32[]{:S(2)}, u32[]{:S(2)}) collective-permute-start(f32[1,36]{1,0:T(1,128)S(1)} %get-tuple-element.5), channel_id=1, source_target_pairs={{0,192},{32,224},{64,128},{96,160},{128,64},{160,96},{192,0},{224,... | collective-permute-start | bytes 440 | tf_op jit(solution)/shard_map/ppermute | solution.py:26
  203.7 32.9 %collective-permute-done.1 = f32[1,36]{1,0:T(1,128)S(1)} collective-permute-done((f32[1,36]{1,0:T(1,128)S(1)}, f32[1,36]{1,0:T(1,128)S(1)}, u32[]{:S(2)}, u32[]{:S(2)}) %collective-permute-start.1) | collective-permute-done | bytes 176 | tf_op jit(solution)/shard_map/ppermute | solution.py:26
  236.7 2.5 collective-permute-start.6
  239.2 1.7 collective-permute-done.6
  241.5 7.7 %fusion.38 = f32[1,144]{1,0:T(1,128)} fusion(f32[4608,1]{0,1:T(1,128)S(1)} %reshape.165, f32[4608,144]{1,0:T(8,128)} %gather_fusion.3, f32[4608,144]{1,0:T(8,128)} %gather_fusion.2, f32[4608]{0:T(1024)S(1)} %fusion.27, pred[4608]{0:T(1024)(128)(4,1)S(1)} %compare_and_fusion), kind=kOutput, calls=%fused_computation.67 | convolution fusion | flops 10616832 | bytes 5350464 | tf_op jit(solution)/shard_map/dot_general | solution.py:79
  249.2 5.6 %reshape.120 = f32[288,4608]{1,0:T(8,128)} reshape(f32[8,36,4608]{2,1,0:T(8,128)} %all-to-all-done) | data formatting | bytes 10616832 | tf_op jit(solution)/shard_map/reshape | solution.py:88
  254.8 6.8 %convolution_bitcast_fusion = f32[1,144,4608]{2,1,0:T(8,128)} fusion(f32[288,4608]{1,0:T(8,128)} %reshape.120, s32[288]{0:T(512)S(1)} %convert_element_type.47), kind=kOutput, calls=%fused_computation.10 | convolution fusion | flops 2293277184 | bytes 7963776 | tf_op jit(solution)/shard_map/dot_general | solution.py:88
  (50 shorter events, 3.1 us)
Async XLA Ops:
  7.2 169.5 %copy-start = (f32[1,4608]{1,0:T(1,128)S(1)}, f32[1,4608]{1,0:T(1,128)}, u32[]{:S(2)}) copy-start(f32[1,4608]{1,0:T(1,128)} %param.13) | copy-start | bytes 55300
  7.2 6.5 %copy-start.5 = (s32[1,4608]{1,0:T(1,128)S(1)}, s32[1,4608]{1,0:T(1,128)}, u32[]{:S(2)}) copy-start(s32[1,4608]{1,0:T(1,128)} %param.15) | copy-start | bytes 55300
  7.2 110.4 %all-gather.3.cloned.1.call-start = ((), (), s32[]{:S(2)}) async-start(), calls=%async_computation.1 | async-start | bytes 9732096 | tf_op jit(solution)/shard_map/all_gather | solution.py:50
  13.7 14.2 %copy-start.6 = (s32[1,144,1]{1,2,0:T(1,128)S(1)}, s32[1,144,1]{1,2,0:T(1,128)}, u32[]{:S(2)}) copy-start(s32[1,144,1]{1,2,0:T(1,128)} %param.16) | copy-start | bytes 1732
  13.8 14.5 %copy-start.4 = (bf16[1,144,1024]{2,1,0:T(8,128)(2,1)S(1)}, bf16[1,144,1024]{2,1,0:T(8,128)(2,1)}, u32[]{:S(2)}) copy-start(bf16[1,144,1024]{2,1,0:T(8,128)(2,1)} %param.10) | copy-start | bytes 884740
  27.9 5.9 %copy-start.2 = (f32[1,1024,1024]{2,1,0:T(8,128)S(1)}, f32[1,1024,1024]{2,1,0:T(8,128)}, u32[]{:S(2)}) copy-start(f32[1,1024,1024]{2,1,0:T(8,128)} %param.12) | copy-start | bytes 12582916
  33.0 0.8 copy-start.3
  117.6 7.1 %copy-start.1 = (bf16[1,4608,1024]{2,1,0:T(8,128)(2,1)S(1)}, bf16[1,4608,1024]{2,1,0:T(8,128)(2,1)}, u32[]{:S(2)}) copy-start(bf16[1,4608,1024]{2,1,0:T(8,128)(2,1)} %all-gather.3.cloned.1.call-done) | copy-start | bytes 28311556
  165.2 5.8 %copy-start.7 = (s32[1,144]{1,0:T(1,128)S(1)}, s32[1,144]{1,0:T(1,128)}, u32[]{:S(2)}) copy-start(s32[1,144]{1,0:T(1,128)} %param.17) | copy-start | bytes 1732
  165.2 84.0 %all-to-all-start = ((f32[8,36,4608]{2,1,0:T(8,128)}), f32[8,36,4608]{2,1,0:T(8,128)}, u32[]{:S(2)}, u32[]{:S(2)}) async-start(f32[8,36,4608]{2,1,0:T(8,128)} %reshape.119), calls=%async_computation | async-start | bytes 11796480 | tf_op jit(solution)/shard_map/all_to_all | solution.py:81
  171.3 29.7 %collective-permute-start = (f32[1,36]{1,0:T(1,128)S(1)}, f32[1,36]{1,0:T(1,128)S(1)}, u32[]{:S(2)}, u32[]{:S(2)}) collective-permute-start(f32[1,36]{1,0:T(1,128)S(1)} %get-tuple-element.10), channel_id=1, source_target_pairs={{0,32},{32,0},{64,96},{96,64},{128,160},{160,128},{192,224},{224,1... | collective-permute-start | bytes 440 | tf_op jit(solution)/shard_map/ppermute | solution.py:26
  171.5 65.1 %collective-permute-start.1 = (f32[1,36]{1,0:T(1,128)S(1)}, f32[1,36]{1,0:T(1,128)S(1)}, u32[]{:S(2)}, u32[]{:S(2)}) collective-permute-start(f32[1,36]{1,0:T(1,128)S(1)} %get-tuple-element.9), channel_id=1, source_target_pairs={{0,64},{32,96},{64,0},{96,32},{128,192},{160,224},{192,128},{224,1... | collective-permute-start | bytes 440 | tf_op jit(solution)/shard_map/ppermute | solution.py:26
  173.1 66.0 %collective-permute-start.2 = (f32[1,36]{1,0:T(1,128)S(1)}, f32[1,36]{1,0:T(1,128)S(1)}, u32[]{:S(2)}, u32[]{:S(2)}) collective-permute-start(f32[1,36]{1,0:T(1,128)S(1)} %get-tuple-element.8), channel_id=1, source_target_pairs={{0,96},{32,64},{64,32},{96,0},{128,224},{160,192},{192,160},{224,1... | collective-permute-start | bytes 440 | tf_op jit(solution)/shard_map/ppermute | solution.py:26
  173.5 65.7 %collective-permute-start.3 = (f32[1,36]{1,0:T(1,128)S(1)}, f32[1,36]{1,0:T(1,128)S(1)}, u32[]{:S(2)}, u32[]{:S(2)}) collective-permute-start(f32[1,36]{1,0:T(1,128)S(1)} %get-tuple-element.7), channel_id=1, source_target_pairs={{0,128},{32,160},{64,192},{96,224},{128,0},{160,32},{192,64},{224,... | collective-permute-start | bytes 440 | tf_op jit(solution)/shard_map/ppermute | solution.py:26
  176.4 62.7 %collective-permute-start.4 = (f32[1,36]{1,0:T(1,128)S(1)}, f32[1,36]{1,0:T(1,128)S(1)}, u32[]{:S(2)}, u32[]{:S(2)}) collective-permute-start(f32[1,36]{1,0:T(1,128)S(1)} %get-tuple-element.6), channel_id=1, source_target_pairs={{0,160},{32,128},{64,224},{96,192},{128,32},{160,0},{192,96},{224,... | collective-permute-start | bytes 440 | tf_op jit(solution)/shard_map/ppermute | solution.py:26
  201.0 38.2 %collective-permute-start.5 = (f32[1,36]{1,0:T(1,128)S(1)}, f32[1,36]{1,0:T(1,128)S(1)}, u32[]{:S(2)}, u32[]{:S(2)}) collective-permute-start(f32[1,36]{1,0:T(1,128)S(1)} %get-tuple-element.5), channel_id=1, source_target_pairs={{0,192},{32,224},{64,128},{96,160},{128,64},{160,96},{192,0},{224,... | collective-permute-start | bytes 440 | tf_op jit(solution)/shard_map/ppermute | solution.py:26
  236.7 4.2 %collective-permute-start.6 = (f32[1,36]{1,0:T(1,128)S(1)}, f32[1,36]{1,0:T(1,128)S(1)}, u32[]{:S(2)}, u32[]{:S(2)}) collective-permute-start(f32[1,36]{1,0:T(1,128)S(1)} %get-tuple-element.4), channel_id=1, source_target_pairs={{0,224},{32,192},{64,160},{96,128},{128,96},{160,64},{192,32},{224... | collective-permute-start | bytes 440 | tf_op jit(solution)/shard_map/ppermute | solution.py:26
Sparse Core Ops, SparseCore 0:
  10.6 106.9 all-gather.2
